TPU v7x, 256 devices: a whole 4x4x8 slice. The times are simulated.
256 devices in a mesh: chan: 8 (over x, y_lo), win: 32 (over y_hi, z, core).
Axes of the slice: x: 4, y: 4 (y_hi: 2, y_lo: 2; y = y_hi * 2 + y_lo), z: 8, core: 2. Of those that a mesh axis runs over, the one named last changes fastest.
Arguments:
- spectra: bfloat16 [768, 32, 2, 4096], P('win', None, None, 'chan'), may hold values from -500 to 500, as said below
- flags: int32 [768], P('win'), may hold values 0 or 1
- pair_table: int32 [8, 8], replicated, may hold values from 0 to 7, each once within a row
Outputs:
- stacks: bfloat16 [32, 2, 4096, 4096], P('win', None, 'chan')
Inputs may be any that keep to these rules, and one draw needn't show every extreme that they name: `spectra`: spectra whose amplitudes vary from window to window, channel to channel and bin to bin. `pair_table`: each row is an ordering of the 8 channel blocks.
All inputs are finite; a program needn't handle non-finite values. No bound on the sum of `flags` on one device may be relied on, other than what follows from the above.
Results may differ from a plain program's by a relative error of at most 0.0067.
Values may be sent and summed in bfloat16 or wider, within the bound.
A program may use at most 64 MiB of HBM per device.

v0:
```python
import math

import jax
import jax.numpy as jnp
from jax import lax
from jax.sharding import PartitionSpec as P

EPSILON = 1e-05


def shifted(value, axis, steps):
    count = lax.axis_size(axis)
    pairs = [(source, (source + steps) % count) for source in range(count)]
    return lax.ppermute(value, axis, pairs)


def place_block(stacks, pair_block, partner, slot_row, group_size, width):
    slot_index = jnp.sum(jnp.where(slot_row == partner, jnp.arange(group_size, dtype=jnp.int32), 0))
    return lax.dynamic_update_slice_in_dim(stacks, pair_block, slot_index * width, 3)


def per_device(spectra, flags, pair_table):
    width = spectra.shape[3]
    group_size = lax.axis_size("chan")
    own_index = lax.axis_index("chan")
    slot_row = pair_table[own_index]
    raw_values = spectra.astype(jnp.float32)
    band_power = jnp.mean(raw_values * raw_values, axis=(1, 2), keepdims=True)
    validity = flags.astype(jnp.float32)[:, None, None, None]
    tempered = (raw_values * lax.rsqrt(band_power + EPSILON) * validity).astype(jnp.bfloat16)
    gathered = lax.all_to_all(tempered, "win", split_axis=1, concat_axis=0, tiled=True)
    all_windows = gathered.shape[0]
    bins_here = gathered.shape[1]
    gathered_wide = gathered.astype(jnp.float32)
    bin_power = jnp.mean(gathered_wide * gathered_wide, axis=(0, 2), keepdims=True)
    whitened = (gathered_wide * lax.rsqrt(bin_power + EPSILON)).astype(jnp.bfloat16)
    stack_scale = 1.0 / math.sqrt(all_windows)
    real_part = whitened[:, :, 0, :]
    imag_part = whitened[:, :, 1, :]
    left_side = jnp.stack(
        [
            jnp.concatenate([real_part, imag_part], axis=-1),
            jnp.concatenate([imag_part, -real_part], axis=-1),
        ],
        axis=2,
    )

    def pair_stack(partner_block):
        product = jnp.einsum(
            "wfpi,wfpj->fij", left_side, partner_block, preferred_element_type=jnp.float32
        )
        return (product * stack_scale).reshape(bins_here, 2, width, width).astype(jnp.bfloat16)

    stacks = jnp.zeros((bins_here, 2, width, group_size * width), jnp.bfloat16)
    stacks = place_block(stacks, pair_stack(whitened), own_index, slot_row, group_size, width)
    moving = whitened
    for step in range(1, group_size):
        moving = shifted(moving, "chan", 1)
        stacks = place_block(
            stacks, pair_stack(moving), (own_index - step) % group_size, slot_row, group_size, width
        )
    return stacks


def solution(mesh):
    return jax.shard_map(
        per_device,
        mesh=mesh,
        in_specs=(P("win", None, None, "chan"), P("win"), P()),
        out_specs=P("win", None, "chan", None),
        check_vma=False,
    )
```

profile of v0, /device:TPU:192, one launch (start us, length us, event | category | flops | bytes accessed | tf_op | source)
XLA Modules:
  0.0 322.5 jit_solution(14393483625651464356)
XLA Ops:
  0.0 3.2 fusion
  3.8 1.8 fusion.2
  5.7 47.5 %all_to_all.4 = bf16[24,32,2,512]{3,0,2,1:T(8,128)(2,1)S(1)} all-to-all(bf16[24,32,2,512]{3,0,2,1:T(8,128)(2,1)S(1)} %fusion.2), channel_id=1, replica_groups=mesh['chan'=8,'win'=32] {'win'}, dimensions={1} | all-to-all | bytes 3145728 | tf_op jit(solution)/shard_map/all_to_all | solution.py:31
  54.3 2.4 copy.23
  56.6 1.8 multiply_reduce_fusion
  58.5 2.1 multiply_convert_fusion
  62.4 38.4 %collective-permute-done = bf16[768,1,2,512]{0,3,2,1:T(8,128)(2,1)S(1)} collective-permute-done((bf16[768,1,2,512]{0,3,2,1:T(8,128)(2,1)S(1)}, bf16[768,1,2,512]{0,3,2,1:T(8,128)(2,1)S(1)}, u32[]{:S(2)}, u32[]{:S(2)}) %collective-permute-start) | collective-permute-done | bytes 1572896 | tf_op jit(solution)/shard_map/ppermute | solution.py:14
  102.0 38.2 %collective-permute-done.1 = bf16[768,1,2,512]{0,3,2,1:T(8,128)(2,1)S(1)} collective-permute-done((bf16[768,1,2,512]{0,3,2,1:T(8,128)(2,1)S(1)}, bf16[768,1,2,512]{0,3,2,1:T(8,128)(2,1)S(1)}, u32[]{:S(2)}, u32[]{:S(2)}) %collective-permute-start.1) | collective-permute-done | bytes 1572896 | tf_op jit(solution)/shard_map/ppermute | solution.py:14
  141.4 37.5 %collective-permute-done.2 = bf16[768,1,2,512]{0,3,2,1:T(8,128)(2,1)} collective-permute-done((bf16[768,1,2,512]{0,3,2,1:T(8,128)(2,1)S(1)}, bf16[768,1,2,512]{0,3,2,1:T(8,128)(2,1)}, u32[]{:S(2)}, u32[]{:S(2)}) %collective-permute-start.2) | collective-permute-done | bytes 1572896 | tf_op jit(solution)/shard_map/ppermute | solution.py:14
  178.9 1.5 fusion.26
  185.4 30.2 %collective-permute-done.3 = bf16[768,1,2,512]{0,3,2,1:T(8,128)(2,1)} collective-permute-done((bf16[768,1,2,512]{0,3,2,1:T(8,128)(2,1)}, bf16[768,1,2,512]{0,3,2,1:T(8,128)(2,1)}, u32[]{:S(2)}, u32[]{:S(2)}) %collective-permute-start.3) | collective-permute-done | bytes 1572896 | tf_op jit(solution)/shard_map/ppermute | solution.py:14
  215.6 1.2 fusion.27
  217.6 1.8 fusion.11
  220.6 30.8 %collective-permute-done.4 = bf16[768,1,2,512]{0,3,2,1:T(8,128)(2,1)S(1)} collective-permute-done((bf16[768,1,2,512]{0,3,2,1:T(8,128)(2,1)}, bf16[768,1,2,512]{0,3,2,1:T(8,128)(2,1)S(1)}, u32[]{:S(2)}, u32[]{:S(2)}) %collective-permute-start.4) | collective-permute-done | bytes 1572896 | tf_op jit(solution)/shard_map/ppermute | solution.py:14
  251.4 1.8 fusion.10
  253.3 1.2 copy-done.8
  254.6 1.8 fusion.9
  256.6 3.2 %fusion.8 = bf16[1024,512]{1,0:T(8,128)(2,1)S(1)} fusion(bf16[768,1,2,512]{0,3,2,1:T(8,128)(2,1)} %collective-permute-done.2, bf16[768,1,1,1024]{0,3,2,1:T(8,128)(2,1)S(1)} %get-tuple-element.16, bf16[768,1,1,1024]{0,3,2,1:T(8,128)(2,1)S(1)} %get-tuple-element.15), kind=kOutput, calls=%fused_computation.19 | convolution fusion | flops 1613234176 | bytes 5767168 | tf_op jit(solution)/shard_map/wfpi,wfpj->fij/dot_general | solution.py:49
  260.0 26.0 %collective-permute-done.5 = bf16[768,1,2,512]{0,3,2,1:T(8,128)(2,1)S(1)} collective-permute-done((bf16[768,1,2,512]{0,3,2,1:T(8,128)(2,1)S(1)}, bf16[768,1,2,512]{0,3,2,1:T(8,128)(2,1)S(1)}, u32[]{:S(2)}, u32[]{:S(2)}) %collective-permute-start.5) | collective-permute-done | bytes 1572896 | tf_op jit(solution)/shard_map/ppermute | solution.py:14
  286.0 3.2 %fusion.7 = bf16[1024,512]{1,0:T(8,128)(2,1)S(1)} fusion(bf16[768,1,2,512]{0,3,2,1:T(8,128)(2,1)} %collective-permute-done.3, bf16[768,1,1,1024]{0,3,2,1:T(8,128)(2,1)S(1)} %get-tuple-element.16, bf16[768,1,1,1024]{0,3,2,1:T(8,128)(2,1)S(1)} %get-tuple-element.15), kind=kOutput, calls=%fused_computation.17 | convolution fusion | flops 1613234176 | bytes 5767168 | tf_op jit(solution)/shard_map/wfpi,wfpj->fij/dot_general | solution.py:49
  289.3 1.8 fusion.6
  291.3 1.8 fusion.5
  293.3 26.3 %collective-permute-done.6 = bf16[768,1,2,512]{0,3,2,1:T(8,128)(2,1)S(1)} collective-permute-done((bf16[768,1,2,512]{0,3,2,1:T(8,128)(2,1)S(1)}, bf16[768,1,2,512]{0,3,2,1:T(8,128)(2,1)S(1)}, u32[]{:S(2)}, u32[]{:S(2)}) %collective-permute-start.6) | collective-permute-done | bytes 1572896 | tf_op jit(solution)/shard_map/ppermute | solution.py:14
  319.7 1.8 fusion.4
  (40 shorter events, 9.8 us)
Async XLA Ops:
  0.0 3.8 %copy-start.4 = (bf16[24,32,2,512]{3,2,1,0:T(2,128)(2,1)S(1)}, bf16[24,32,2,512]{3,2,1,0:T(2,128)(2,1)}, u32[]{:S(2)}) copy-start(bf16[24,32,2,512]{3,2,1,0:T(2,128)(2,1)} %param.3) | copy-start | bytes 4718596
  53.1 1.2 copy-start
  60.6 1.1 copy-start.1
  61.7 39.1 %collective-permute-start = (bf16[768,1,2,512]{0,3,2,1:T(8,128)(2,1)S(1)}, bf16[768,1,2,512]{0,3,2,1:T(8,128)(2,1)S(1)}, u32[]{:S(2)}, u32[]{:S(2)}) collective-permute-start(bf16[768,1,2,512]{0,3,2,1:T(8,128)(2,1)S(1)} %multiply_convert_fusion), channel_id=1, source_target_pairs={{0,32},{32,64},{64,96},{96,128},{128,160},{160,192},{192,224},{224... | collective-permute-start | bytes 4718600 | tf_op jit(solution)/shard_map/ppermute | solution.py:14
  100.8 1.2 copy-start.5
  102.0 38.2 %collective-permute-start.1 = (bf16[768,1,2,512]{0,3,2,1:T(8,128)(2,1)S(1)}, bf16[768,1,2,512]{0,3,2,1:T(8,128)(2,1)S(1)}, u32[]{:S(2)}, u32[]{:S(2)}) collective-permute-start(bf16[768,1,2,512]{0,3,2,1:T(8,128)(2,1)S(1)} %collective-permute-done), channel_id=1, source_target_pairs={{0,32},{32,64},{64,96},{96,128},{128,160},{160,192},{192,224},{224... | collective-permute-start | bytes 4718600 | tf_op jit(solution)/shard_map/ppermute | solution.py:14
  140.2 1.1 copy-start.7
  141.4 37.5 %collective-permute-start.2 = (bf16[768,1,2,512]{0,3,2,1:T(8,128)(2,1)S(1)}, bf16[768,1,2,512]{0,3,2,1:T(8,128)(2,1)}, u32[]{:S(2)}, u32[]{:S(2)}) collective-permute-start(bf16[768,1,2,512]{0,3,2,1:T(8,128)(2,1)S(1)} %collective-permute-done.1), channel_id=1, source_target_pairs={{0,32},{32,64},{64,96},{96,128},{128,160},{160,192},{192,224},{224... | collective-permute-start | bytes 4718600 | tf_op jit(solution)/shard_map/ppermute | solution.py:14
  178.9 36.8 %collective-permute-start.3 = (bf16[768,1,2,512]{0,3,2,1:T(8,128)(2,1)}, bf16[768,1,2,512]{0,3,2,1:T(8,128)(2,1)}, u32[]{:S(2)}, u32[]{:S(2)}) collective-permute-start(bf16[768,1,2,512]{0,3,2,1:T(8,128)(2,1)} %collective-permute-done.2), channel_id=1, source_target_pairs={{0,32},{32,64},{64,96},{96,128},{128,160},{160,192},{192,224},{224... | collective-permute-start | bytes 4718600 | tf_op jit(solution)/shard_map/ppermute | solution.py:14
  185.4 31.4 %copy-start.2 = (bf16[768,1,2,512]{0,3,2,1:T(8,128)(2,1)S(1)}, bf16[768,1,2,512]{0,3,2,1:T(8,128)(2,1)}, u32[]{:S(2)}) copy-start(bf16[768,1,2,512]{0,3,2,1:T(8,128)(2,1)} %copy-done.1) | copy-start | bytes 4718596
  215.6 35.7 %collective-permute-start.4 = (bf16[768,1,2,512]{0,3,2,1:T(8,128)(2,1)}, bf16[768,1,2,512]{0,3,2,1:T(8,128)(2,1)S(1)}, u32[]{:S(2)}, u32[]{:S(2)}) collective-permute-start(bf16[768,1,2,512]{0,3,2,1:T(8,128)(2,1)} %collective-permute-done.3), channel_id=1, source_target_pairs={{0,32},{32,64},{64,96},{96,128},{128,160},{160,192},{192,224},{224... | collective-permute-start | bytes 4718600 | tf_op jit(solution)/shard_map/ppermute | solution.py:14
  220.4 30.9 %copy-start.6 = (bf16[768,1,2,512]{0,3,2,1:T(8,128)(2,1)S(1)}, bf16[768,1,2,512]{0,3,2,1:T(8,128)(2,1)}, u32[]{:S(2)}) copy-start(bf16[768,1,2,512]{0,3,2,1:T(8,128)(2,1)} %copy-done.5) | copy-start | bytes 4718596
  251.4 34.6 %collective-permute-start.5 = (bf16[768,1,2,512]{0,3,2,1:T(8,128)(2,1)S(1)}, bf16[768,1,2,512]{0,3,2,1:T(8,128)(2,1)S(1)}, u32[]{:S(2)}, u32[]{:S(2)}) collective-permute-start(bf16[768,1,2,512]{0,3,2,1:T(8,128)(2,1)S(1)} %collective-permute-done.4), channel_id=1, source_target_pairs={{0,32},{32,64},{64,96},{96,128},{128,160},{160,192},{192,224},{224... | collective-permute-start | bytes 4718600 | tf_op jit(solution)/shard_map/ppermute | solution.py:14
  253.2 1.4 copy-start.8
  286.0 33.7 %collective-permute-start.6 = (bf16[768,1,2,512]{0,3,2,1:T(8,128)(2,1)S(1)}, bf16[768,1,2,512]{0,3,2,1:T(8,128)(2,1)S(1)}, u32[]{:S(2)}, u32[]{:S(2)}) collective-permute-start(bf16[768,1,2,512]{0,3,2,1:T(8,128)(2,1)S(1)} %collective-permute-done.5), channel_id=1, source_target_pairs={{0,32},{32,64},{64,96},{96,128},{128,160},{160,192},{192,224},{224... | collective-permute-start | bytes 4718600 | tf_op jit(solution)/shard_map/ppermute | solution.py:14
  293.3 28.2 %copy-start.3 = (bf16[1,2,512,4096]{3,2,1,0:T(8,128)(2,1)}, bf16[1,2,512,4096]{3,2,1,0:T(8,128)(2,1)S(1)}, u32[]{:S(2)}) copy-start(bf16[1,2,512,4096]{3,2,1,0:T(8,128)(2,1)S(1)} %constant_dynamic-update-slice_fusion.1) | copy-start | bytes 25165828
where the time goes:
time: 323 us
  waiting for transfers between devices  227 us (70%)
  blocking collectives  47.5 us (15%)
  matrix products  17.3 us (5%)
  other arithmetic  13.3 us (4%)
  local copies, waits for them, and re-layouts  11 us (3%)
  between operations  5.27 us (2%)
    ppermute x7, waiting for transfers between devices, shifted(): return lax.ppermute(value, axis, pairs)  227 us
    all_to_all x1, blocking collectives, per_device(): lax.all_to_all(tempered, 'win', split_axis=1, concat_axis=0, tiled=True)  47.5 us
    dot_general x8, matrix products, pair_stack(): jnp.einsum('wfpi,wfpj->fij', left_side, partner_block, preferred_element_...  17.3 us
  transfers between devices with their start and end apart: 7, of which 7 were waited for; matrix products, arithmetic and copies ran while one was open for 7% of the time, Pallas kernels for 0%

commit v1 on v0

v1 whole, which is shorter than its diff:
```python
import functools
import math

import jax
import jax.numpy as jnp
from jax import lax
from jax.experimental import pallas as pl
from jax.experimental.pallas import tpu as pltpu
from jax.sharding import PartitionSpec as P

EPSILON = 1e-05
MESH = pl.DeviceIdType.MESH

NX = 4
NZ = 8
GROUPS = 8
OFFSETS = (0, 1, -1, 2, -2, 3, -3, 4)
NBLK = 8
HALF = 96
CUT_LO = 64
CUT_HI = 144


def gather_stack_kernel(
    chunk_rows,
    tempered,
    prod,
    x_all,
    acc,
    left,
    colpow,
    rowpow,
    a2a_send,
    a2a_recv,
    local_sem,
    ag_send,
    recv1,
    recv2,
    recv3,
    *,
    windows,
):
    c = lax.axis_index("chan")
    w = lax.axis_index("win")
    x, yl = c // 2, c % 2
    yh, z, core = w // 16, (w // 2) % NZ, w % 2
    xp = (x + 1 + 2 * core) % NX
    xm = (x + 3 + 2 * core) % NX
    x2 = (x + 2) % NX

    def src(xx, yy):
        return 2 * xx + yy

    own = src(x, yl)
    pair = src(x, 1 - yl)
    dev_p = (src(xp, yl), w)
    dev_m = (src(xm, yl), w)
    dev_y = (pair, w)

    def peer(zz, other_half, other_core):
        cc = c if not other_half else pair
        hh = yh if not other_half else 1 - yh
        kk = core if not other_core else 1 - core
        return (cc, hh * 16 + zz * 2 + kk)

    barrier = pltpu.get_barrier_semaphore()
    count = 0
    for off in OFFSETS:
        zz = (z - off) % NZ
        for other_half in (0, 1):
            for other_core in (0, 1):
                if off == 0 and not other_half and not other_core:
                    continue
                pl.semaphore_signal(
                    barrier, inc=1, device_id=peer(zz, other_half, other_core), device_id_type=MESH
                )
                count += 1
    for dev in (dev_p, dev_m, dev_y):
        pl.semaphore_signal(barrier, inc=1, device_id=dev, device_id_type=MESH)
        count += 1
    pl.semaphore_wait(barrier, count)

    local = None
    for g, off in enumerate(OFFSETS):
        zz = (z - off) % NZ
        for other_half in (0, 1):
            for other_core in (0, 1):
                dev = peer(zz, other_half, other_core)
                row = other_half * HALF + core * chunk_rows
                row = pl.multiple_of(row, 16)
                if off == 0 and not other_half and not other_core:
                    local = pltpu.make_async_copy(
                        tempered.at[w], x_all.at[own, g, pl.ds(row, chunk_rows)], local_sem
                    )
                    local.start()
                    continue
                entry = own if not other_half else pair
                pltpu.make_async_remote_copy(
                    src_ref=tempered.at[dev[1]],
                    dst_ref=x_all.at[entry, g, pl.ds(row, chunk_rows)],
                    send_sem=a2a_send,
                    recv_sem=a2a_recv.at[g],
                    device_id=dev,
                    device_id_type=MESH,
                ).start()

    def send(s, g, lo, hi, recv_sem, dev):
        ref = x_all.at[s, g, pl.ds(lo, hi - lo)]
        pltpu.make_async_remote_copy(
            src_ref=ref,
            dst_ref=ref,
            send_sem=ag_send,
            recv_sem=recv_sem,
            device_id=dev,
            device_id_type=MESH,
        ).start()

    def await_rows(rows, sem):
        ref = x_all.at[0, 0, pl.ds(0, rows)]
        pltpu.make_async_copy(ref, ref, sem).wait()

    full = 2 * HALF

    def phase1(g):
        if g == 0:
            local.wait()
            await_rows(full - chunk_rows, a2a_recv.at[g])
        else:
            await_rows(full, a2a_recv.at[g])
        send(own, g, 0, full, recv1.at[g, 0], dev_p)
        send(own, g, 0, full, recv1.at[g, 1], dev_m)
        send(own, g, 0, full, recv1.at[g, 2], dev_y)

    def phase2(g):
        s_m, s_p = src(xm, yl), src(xp, yl)
        await_rows(full, recv1.at[g, 0])
        send(s_m, g, 0, HALF, recv2.at[g, 0], dev_p)
        await_rows(full, recv1.at[g, 1])
        send(s_p, g, HALF, full, recv2.at[g, 1], dev_m)
        send(s_m, g, CUT_LO, CUT_HI, recv2.at[g, 2], dev_y)
        send(s_p, g, CUT_LO, CUT_HI, recv2.at[g, 3], dev_y)
        await_rows(full, recv1.at[g, 2])
        send(pair, g, 0, CUT_LO, recv2.at[g, 4], dev_p)
        send(pair, g, CUT_HI, full, recv2.at[g, 5], dev_m)
        send(pair, g, CUT_HI, full, recv2.at[g, 4], dev_p)
        send(pair, g, 0, CUT_LO, recv2.at[g, 5], dev_m)

    cut = CUT_HI - CUT_LO

    def phase3(g):
        s_m, s_p = src(xm, 1 - yl), src(xp, 1 - yl)
        await_rows(HALF, recv2.at[g, 0])
        await_rows(HALF, recv2.at[g, 1])
        send(src(x2, yl), g, CUT_LO, CUT_HI, recv3.at[g, 0], dev_y)
        await_rows(full - cut, recv2.at[g, 4])
        send(s_m, g, 0, CUT_LO, recv3.at[g, 1], dev_p)
        await_rows(full - cut, recv2.at[g, 5])
        send(s_p, g, CUT_HI, full, recv3.at[g, 2], dev_m)
        await_rows(cut, recv2.at[g, 2])
        await_rows(cut, recv2.at[g, 3])

    def arrived(g):
        await_rows(cut, recv3.at[g, 0])
        await_rows(CUT_LO, recv3.at[g, 1])
        await_rows(full - CUT_HI, recv3.at[g, 2])

    half_rows = 2 * HALF
    width = x_all.shape[3]

    def block_rows(b, g0):
        other = b + 1 - 2 * (b % 2)
        same = x_all[b, g0 : g0 + 2, 0:HALF, :].reshape(half_rows, width)
        cross = x_all[other, g0 : g0 + 2, HALF:full, :].reshape(half_rows, width)
        return jnp.concatenate([same, cross], axis=0)

    def stack_step(g0, first, last):
        mine = block_rows(own, g0).astype(jnp.float32)
        parts = mine.reshape(2 * half_rows // chunk_rows, chunk_rows, width)
        h = chunk_rows // 2
        swapped = jnp.concatenate([parts[:, h:, :], -parts[:, :h, :]], axis=1)
        swapped = swapped.reshape(2 * half_rows, width)
        re_t = mine.T
        left[0:width, :] = re_t.astype(jnp.bfloat16)
        left[width:, :] = swapped.T.astype(jnp.bfloat16)
        squares = re_t * re_t
        lanes = squares[:, 0:128]
        for k in range(128, 2 * half_rows, 128):
            lanes = lanes + squares[:, k : k + 128]
        if first:
            rowpow[...] = lanes
        else:
            rowpow[...] += lanes
        mean = 1.0 / (2 * windows)
        if last:
            total = jnp.sum(rowpow[...], axis=1, keepdims=True) * mean
            row_scale = lax.rsqrt(total + EPSILON) * (1.0 / math.sqrt(windows))
            rowpow[...] = jnp.broadcast_to(row_scale, rowpow.shape)

        def body(b, carry):
            right = block_rows(b, g0)
            wide = right.astype(jnp.float32)
            sq = jnp.sum((wide * wide).reshape(2 * half_rows // 8, 8, width), axis=0)
            if not first:
                sq = sq + colpow[b]
            if not last:
                colpow[b] = sq
            else:
                col = lax.rsqrt(jnp.sum(sq, axis=0, keepdims=True) * mean + EPSILON)
            for part in (0, 1):
                product = jnp.dot(
                    left[part * width : (part + 1) * width, :], right, preferred_element_type=jnp.float32
                )
                if not first:
                    product = product + acc[b, part]
                if not last:
                    acc[b, part] = product
                else:
                    prod[b, part] = (product * rowpow[:, 0:1] * col).astype(jnp.bfloat16)
            return carry

        lax.fori_loop(0, NBLK, body, 0)

    for it in range(GROUPS + 3):
        if it < GROUPS:
            phase1(it)
        if 1 <= it < GROUPS + 1:
            phase2(it - 1)
        if 2 <= it < GROUPS + 2:
            phase3(it - 2)
        if it >= 3:
            done = it - 3
            arrived(done)
            if done % 2 == 1:
                stack_step(done - 1, done == 1, done == GROUPS - 1)

    sent = tempered.at[0:31]
    pltpu.make_async_copy(sent, sent, a2a_send).wait()
    sent = x_all.at[0:7]
    pltpu.make_async_copy(sent, sent, ag_send).wait()


def place_kernel(table, prod, out, sem):
    c = lax.axis_index("chan")
    width = prod.shape[2]
    copies = []
    for s in range(NBLK):
        copy = pltpu.make_async_copy(
            prod.at[table[c, s]], out.at[0, :, :, pl.ds(s * width, width)], sem.at[s]
        )
        copy.start()
        copies.append(copy)
    for copy in copies:
        copy.wait()


def per_device(spectra, flags, pair_table):
    local, bins, parts, width = spectra.shape
    windows = local * lax.axis_size("win")
    raw = spectra.astype(jnp.float32)
    band = jnp.mean(raw * raw, axis=(1, 2), keepdims=True)
    validity = flags.astype(jnp.float32)[:, None, None, None]
    tempered = (raw * lax.rsqrt(band + EPSILON) * validity).astype(jnp.bfloat16)
    chunk_rows = local * parts
    tempered = tempered.transpose(1, 2, 0, 3).reshape(bins, chunk_rows, width)

    vmem = pl.BlockSpec(memory_space=pltpu.VMEM)
    prod = pl.pallas_call(
        functools.partial(gather_stack_kernel, chunk_rows, windows=windows),
        out_shape=jax.ShapeDtypeStruct((NBLK, 2, width, width), jnp.bfloat16),
        in_specs=[vmem],
        out_specs=vmem,
        scratch_shapes=[
            pltpu.VMEM((NBLK, GROUPS, 2 * HALF, width), jnp.bfloat16),
            pltpu.VMEM((NBLK, 2, width, width), jnp.float32),
            pltpu.VMEM((2 * width, 4 * HALF), jnp.bfloat16),
            pltpu.VMEM((NBLK, 8, width), jnp.float32),
            pltpu.VMEM((width, 128), jnp.float32),
            pltpu.SemaphoreType.DMA,
            pltpu.SemaphoreType.DMA((GROUPS,)),
            pltpu.SemaphoreType.DMA,
            pltpu.SemaphoreType.DMA,
            pltpu.SemaphoreType.DMA((GROUPS, 3)),
            pltpu.SemaphoreType.DMA((GROUPS, 6)),
            pltpu.SemaphoreType.DMA((GROUPS, 3)),
        ],
        compiler_params=pltpu.CompilerParams(
            collective_id=0, has_side_effects=True, vmem_limit_bytes=56 * 1024 * 1024
        ),
        name="gather_stack",
    )(tempered)

    return pl.pallas_call(
        place_kernel,
        out_shape=jax.ShapeDtypeStruct((1, 2, width, NBLK * width), jnp.bfloat16),
        in_specs=[pl.BlockSpec(memory_space=pltpu.SMEM), vmem],
        out_specs=pl.BlockSpec(memory_space=pl.ANY),
        scratch_shapes=[pltpu.SemaphoreType.DMA((NBLK,))],
        name="place_blocks",
    )(pair_table, prod)


def solution(mesh):
    return jax.shard_map(
        per_device,
        mesh=mesh,
        in_specs=(P("win", None, None, "chan"), P("win"), P()),
        out_specs=P("win", None, "chan", None),
        check_vma=False,
    )
```

time: 323 us -> 132 us (0.41)
  the two profiles are of different devices: /device:TPU:192 before, /device:TPU:1 now
where the time goes in v1:
time: 132 us; the launch traced here: 131 us
  Pallas kernels  122 us (92%)
  other arithmetic  7.08 us (5%)
  local copies, waits for them, and re-layouts  2.43 us (2%)
    pallas_call x1, Pallas kernels, per_device(): pl.pallas_call(functools.partial(gather_stack_kernel, chunk_rows, windows...  115 us
    pallas_call x1, Pallas kernels, per_device(): pl.pallas_call(place_kernel, out_shape=jax.ShapeDtypeStruct((1, 2, width,...  6.77 us
    transpose x1, other arithmetic, per_device(): tempered = tempered.transpose(1, 2, 0, 3).reshape(bins, chunk_rows, width)  3.3 us
    reduce_sum x1, other arithmetic, per_device(): band = jnp.mean(raw * raw, axis=(1, 2), keepdims=True)  3.11 us

profile of v1, /device:TPU:1, one launch (start us, length us, event | category | flops | bytes accessed | tf_op | source)
XLA Modules:
  0.0 131.3 jit_solution(17945441337527004025)
XLA Ops:
  0.0 0.7 convert_element_type.10
  0.7 3.1 %fusion = f32[24,512]{1,0:T(8,128)S(1)} fusion(bf16[24,32,2,512]{3,2,1,0:T(2,128)(2,1)} %param.3), kind=kLoop, calls=%fused_computation.2 | loop fusion | flops 2347008 | bytes 1622016 | tf_op jit(solution)/shard_map/reduce_sum | solution.py:260
  3.8 3.3 %fusion.3 = bf16[32,2,24,512]{3,1,0,2:T(2,128)(2,1)S(1)} fusion(f32[24]{0:T(128)S(1)} %convert_element_type.10, f32[24,512]{1,0:T(8,128)S(1)} %add_rsqrt_fusion, bf16[24,32,2,512]{3,2,1,0:T(2,128)(2,1)} %param.3), kind=kLoop, calls=%fused_computation.5 | loop fusion | flops 3145728 | bytes 3194976 | tf_op jit(solution)/shard_map/transpose | solution.py:264
  7.1 2.4 %copy.4 = bf16[32,2,24,512]{3,2,1,0:T(8,128)(2,1)} copy(bf16[32,2,24,512]{3,1,0,2:T(2,128)(2,1)S(1)} %fusion.3) | data formatting | bytes 3145728 | tf_op jit(solution)/shard_map/transpose | solution.py:264
  9.5 115.0 %gather_stack.1.prod = bf16[8,2,512,512]{3,2,1,0:T(8,128)(2,1)} custom-call(bf16[32,48,512]{2,1,0:T(8,128)(2,1)} %bitcast.3), custom_call_target="tpu_custom_call" | custom-call | tf_op jit(solution)/shard_map/gather_stack/pallas_call | solution.py:267
  124.6 6.8 %place_blocks.1 = bf16[1,2,512,4096]{3,2,1,0:T(8,128)(2,1)} custom-call(s32[8,8]{1,0:T(8,128)} %table.1, bf16[8,2,512,512]{3,2,1,0:T(8,128)(2,1)} %gather_stack.1.prod), custom_call_target="tpu_custom_call" | custom-call | tf_op jit(solution)/shard_map/place_blocks/pallas_call | solution.py:292
  (1 shorter events, 0.0 us)

commit v2 on v1

v2 whole, which is shorter than its diff:
```python
import functools
import math

import jax
import jax.numpy as jnp
from jax import lax
from jax.experimental import pallas as pl
from jax.experimental.pallas import tpu as pltpu
from jax.sharding import PartitionSpec as P

EPSILON = 1e-05
MESH = pl.DeviceIdType.MESH

NX = 4
NZ = 8
GROUPS = 8
OFFSETS = (0, 1, -1, 2, -2, 3, -3, 4)
NBLK = 8
HALF = 96
CUT_LO = 64
CUT_HI = (144, 160, 144, 160, 144, 160, 144, 144)
STEPS = ((0, 2), (2, 2), (4, 2), (6, 2))
GATE = 3


def block_rows(x_all, b, g0, groups):
    other = b + 1 - 2 * (b % 2)
    rows, width = groups * HALF, x_all.shape[3]
    same = x_all[b, g0 : g0 + groups, 0:HALF, :].reshape(rows, width)
    cross = x_all[other, g0 : g0 + groups, HALF : 2 * HALF, :].reshape(rows, width)
    return jnp.concatenate([same, cross], axis=0)


def build_left(x_all, own, g0, groups, chunk_rows, left, rowpow, first):
    rows, width = 2 * groups * HALF, x_all.shape[3]
    mine = block_rows(x_all, own, g0, groups).astype(jnp.float32)
    parts = mine.reshape(rows // chunk_rows, chunk_rows, width)
    h = chunk_rows // 2
    swapped = jnp.concatenate([parts[:, h:, :], -parts[:, :h, :]], axis=1).reshape(rows, width)
    re_t = mine.T
    left[0:width, 0:rows] = re_t.astype(jnp.bfloat16)
    left[width:, 0:rows] = swapped.T.astype(jnp.bfloat16)
    squares = re_t * re_t
    lanes = squares[:, 0:128]
    for k in range(128, rows, 128):
        lanes = lanes + squares[:, k : k + 128]
    rowpow[...] = lanes if first else rowpow[...] + lanes


def squares_of(right):
    wide = right.astype(jnp.float32)
    return jnp.sum((wide * wide).reshape(right.shape[0] // 8, 8, right.shape[1]), axis=0)


def gather_stack_kernel(
    flags,
    spectra,
    x_all,
    acc,
    left,
    colpow,
    rowpow,
    wide,
    tempered,
    a2a_send,
    a2a_recv,
    local_sem,
    ag_send,
    recv1,
    recv2,
    recv3,
):
    local_windows = spectra.shape[0]
    bins = wide.shape[0]
    chunk_rows = tempered.shape[1]
    c = lax.axis_index("chan")
    w = lax.axis_index("win")
    x, yl = c // 2, c % 2
    yh, z, core = w // 16, (w // 2) % NZ, w % 2
    xp = (x + 1 + 2 * core) % NX
    xm = (x + 3 + 2 * core) % NX
    x2 = (x + 2) % NX

    def src(xx, yy):
        return 2 * xx + yy

    own = src(x, yl)
    pair = src(x, 1 - yl)
    dev_p = (src(xp, yl), w)
    dev_m = (src(xm, yl), w)
    dev_y = (pair, w)

    def peer(zz, other_half, other_core):
        cc = c if not other_half else pair
        hh = yh if not other_half else 1 - yh
        kk = core if not other_core else 1 - core
        return (cc, hh * 16 + zz * 2 + kk)

    barrier = pltpu.get_barrier_semaphore()
    count = 0
    for off in OFFSETS:
        zz = (z - off) % NZ
        for other_half in (0, 1):
            for other_core in (0, 1):
                if off == 0 and not other_half and not other_core:
                    continue
                pl.semaphore_signal(
                    barrier, inc=1, device_id=peer(zz, other_half, other_core), device_id_type=MESH
                )
                count += 1
    for dev in (dev_p, dev_m, dev_y):
        pl.semaphore_signal(barrier, inc=1, device_id=dev, device_id_type=MESH)
        count += 1

    odd = lax.broadcasted_iota(jnp.int32, (8, 128), 0) % 2

    def temper(i, carry):
        raw = spectra[i].astype(jnp.float32).reshape(bins, 8, 128)
        power = jnp.sum(raw * raw, axis=0)
        power = power + jnp.where(odd == 0, pltpu.roll(power, 7, 0), pltpu.roll(power, 1, 0))
        scale = lax.rsqrt(power * (1.0 / (2 * bins)) + EPSILON) * flags[i].astype(jnp.float32)
        wide[:, pl.ds(pl.multiple_of(i * 8, 8), 8), :] = raw * scale
        return carry

    lax.fori_loop(0, local_windows, temper, 0)

    def arrange(b):
        for tile in range(4):
            re = wide[b, pl.ds(2 * tile, local_windows, stride=8), :]
            im = wide[b, pl.ds(2 * tile + 1, local_windows, stride=8), :]
            both = jnp.concatenate([re, im], axis=0)
            tempered[b, :, tile * 128 : (tile + 1) * 128] = both.astype(jnp.bfloat16)

    pl.semaphore_wait(barrier, count)

    local = None
    for g, off in enumerate(OFFSETS):
        zz = (z - off) % NZ
        for other_half in (0, 1):
            for other_core in (0, 1):
                dev = peer(zz, other_half, other_core)
                arrange(dev[1])
                row = other_half * HALF + core * chunk_rows
                row = pl.multiple_of(row, 16)
                if off == 0 and not other_half and not other_core:
                    local = pltpu.make_async_copy(
                        tempered.at[w], x_all.at[own, g, pl.ds(row, chunk_rows)], local_sem
                    )
                    local.start()
                    continue
                entry = own if not other_half else pair
                pltpu.make_async_remote_copy(
                    src_ref=tempered.at[dev[1]],
                    dst_ref=x_all.at[entry, g, pl.ds(row, chunk_rows)],
                    send_sem=a2a_send,
                    recv_sem=a2a_recv.at[g],
                    device_id=dev,
                    device_id_type=MESH,
                ).start()

    def send(s, g, lo, hi, recv_sem, dev):
        ref = x_all.at[s, g, pl.ds(lo, hi - lo)]
        pltpu.make_async_remote_copy(
            src_ref=ref,
            dst_ref=ref,
            send_sem=ag_send,
            recv_sem=recv_sem,
            device_id=dev,
            device_id_type=MESH,
        ).start()

    def await_rows(rows, sem):
        ref = x_all.at[0, 0, pl.ds(0, rows)]
        pltpu.make_async_copy(ref, ref, sem).wait()

    full = 2 * HALF

    def phase1(g):
        if g == 0:
            local.wait()
            await_rows(full - chunk_rows, a2a_recv.at[g])
        else:
            await_rows(full, a2a_recv.at[g])
        send(own, g, 0, full, recv1.at[g, 0], dev_p)
        send(own, g, 0, full, recv1.at[g, 1], dev_m)
        send(own, g, 0, full, recv1.at[g, 2], dev_y)

    def phase2(g):
        s_m, s_p = src(xm, yl), src(xp, yl)
        await_rows(full, recv1.at[g, 0])
        send(s_m, g, 0, HALF, recv2.at[g, 0], dev_p)
        await_rows(full, recv1.at[g, 1])
        send(s_p, g, HALF, full, recv2.at[g, 1], dev_m)
        send(s_m, g, CUT_LO, CUT_HI[g], recv2.at[g, 2], dev_y)
        send(s_p, g, CUT_LO, CUT_HI[g], recv2.at[g, 3], dev_y)
        await_rows(full, recv1.at[g, 2])
        send(pair, g, 0, CUT_LO, recv2.at[g, 4], dev_p)
        send(pair, g, CUT_HI[g], full, recv2.at[g, 5], dev_m)
        send(pair, g, CUT_HI[g], full, recv2.at[g, 4], dev_p)
        send(pair, g, 0, CUT_LO, recv2.at[g, 5], dev_m)

    def phase3(g):
        s_m, s_p = src(xm, 1 - yl), src(xp, 1 - yl)
        cut = CUT_HI[g] - CUT_LO
        await_rows(HALF, recv2.at[g, 0])
        await_rows(HALF, recv2.at[g, 1])
        send(src(x2, yl), g, CUT_LO, CUT_HI[g], recv3.at[g, 0], dev_y)
        await_rows(full - cut, recv2.at[g, 4])
        send(s_m, g, 0, CUT_LO, recv3.at[g, 1], dev_p)
        await_rows(full - cut, recv2.at[g, 5])
        send(s_p, g, CUT_HI[g], full, recv3.at[g, 2], dev_m)
        await_rows(cut, recv2.at[g, 2])
        await_rows(cut, recv2.at[g, 3])

    def arrived(g):
        await_rows(CUT_HI[g] - CUT_LO, recv3.at[g, 0])
        await_rows(CUT_LO, recv3.at[g, 1])
        await_rows(full - CUT_HI[g], recv3.at[g, 2])

    width = x_all.shape[3]

    def stack_step(g0, groups, first):
        rows = groups * full
        build_left(x_all, own, g0, groups, chunk_rows, left, rowpow, first)

        def body(b, carry):
            right = block_rows(x_all, b, g0, groups)
            squares = squares_of(right)
            colpow[b] = squares if first else colpow[b] + squares
            for part in (0, 1):
                product = jnp.dot(
                    left[part * width : (part + 1) * width, 0:rows],
                    right,
                    preferred_element_type=jnp.float32,
                )
                acc[b, part] = product if first else acc[b, part] + product
            return carry

        lax.fori_loop(0, NBLK, body, 0)

    for it in range(GROUPS + GATE):
        if it < GROUPS:
            phase1(it)
        if 1 <= it < GROUPS + 1:
            phase2(it - 1)
        if 2 <= it < GROUPS + 2:
            phase3(it - 2)
        if it == GROUPS + 1:
            pass
        if it >= GATE:
            done = it - GATE
            arrived(done)
            for g0, groups in STEPS[:-1]:
                if done == g0 + groups - 1:
                    stack_step(g0, groups, g0 == 0)
            if done == STEPS[-1][0] - 1:
                g0, groups = STEPS[-1]
                build_left(x_all, own, g0, groups, chunk_rows, left, rowpow, False)

    sent = tempered.at[0:31]
    pltpu.make_async_copy(sent, sent, a2a_send).wait()
    sent = x_all.at[0:7]
    pltpu.make_async_copy(sent, sent, ag_send).wait()


def finish_kernel(table, x_all, acc, left, colpow, rowpow, out, buf, sem, *, windows):
    c = lax.axis_index("chan")
    width = x_all.shape[3]
    g0, groups = STEPS[-1]
    rows = 2 * groups * HALF
    mean = 1.0 / (2 * windows)
    row = lax.rsqrt(jnp.sum(rowpow[...], axis=1, keepdims=True) * mean + EPSILON)
    row = row * (1.0 / math.sqrt(windows))

    def copy(s):
        return pltpu.make_async_copy(
            buf.at[s % 2], out.at[0, :, :, pl.ds(s * width, width)], sem.at[s % 2]
        )

    for s in range(NBLK):
        b = table[c, s]
        right = block_rows(x_all, b, g0, groups)
        power = jnp.sum(colpow[b] + squares_of(right), axis=0, keepdims=True)
        col = lax.rsqrt(power * mean + EPSILON)
        if s >= 2:
            copy(s - 2).wait()
        for part in (0, 1):
            product = jnp.dot(
                left[part * width : (part + 1) * width, 0:rows],
                right,
                preferred_element_type=jnp.float32,
            )
            product = product + acc[b, part]
            buf[s % 2, part] = (product * row * col).astype(jnp.bfloat16)
        copy(s).start()
    copy(NBLK - 2).wait()
    copy(NBLK - 1).wait()


def per_device(spectra, flags, pair_table):
    local, bins, parts, width = spectra.shape
    windows = local * lax.axis_size("win")
    chunk_rows = local * parts
    tiles = width // 128
    rows = spectra.reshape(local, bins, parts, tiles, 128).transpose(0, 1, 3, 2, 4)
    rows = rows.reshape(local, bins * tiles * parts, 128)

    vmem = pl.BlockSpec(memory_space=pltpu.VMEM)
    smem = pl.BlockSpec(memory_space=pltpu.SMEM)
    left_rows = 2 * HALF * max(n for _, n in STEPS)
    kept = pl.pallas_call(
        gather_stack_kernel,
        out_shape=[
            pltpu.VMEM((NBLK, GROUPS, 2 * HALF, width), jnp.bfloat16),
            pltpu.VMEM((NBLK, 2, width, width), jnp.float32),
            pltpu.VMEM((2 * width, left_rows), jnp.bfloat16),
            pltpu.VMEM((NBLK, 8, width), jnp.float32),
            pltpu.VMEM((width, 128), jnp.float32),
        ],
        in_specs=[smem, vmem],
        out_specs=[vmem] * 5,
        scratch_shapes=[
            pltpu.VMEM((bins, local * 8, 128), jnp.float32),
            pltpu.VMEM((bins, chunk_rows, width), jnp.bfloat16),
            pltpu.SemaphoreType.DMA,
            pltpu.SemaphoreType.DMA((GROUPS,)),
            pltpu.SemaphoreType.DMA,
            pltpu.SemaphoreType.DMA,
            pltpu.SemaphoreType.DMA((GROUPS, 3)),
            pltpu.SemaphoreType.DMA((GROUPS, 6)),
            pltpu.SemaphoreType.DMA((GROUPS, 3)),
        ],
        compiler_params=pltpu.CompilerParams(
            collective_id=0, has_side_effects=True, vmem_limit_bytes=10 * 1024 * 1024
        ),
        name="gather_stack",
    )(flags, rows)

    return pl.pallas_call(
        functools.partial(finish_kernel, windows=windows),
        out_shape=jax.ShapeDtypeStruct((1, 2, width, NBLK * width), jnp.bfloat16),
        in_specs=[smem] + [vmem] * 5,
        out_specs=pl.BlockSpec(memory_space=pl.ANY),
        scratch_shapes=[
            pltpu.VMEM((2, 2, width, width), jnp.bfloat16),
            pltpu.SemaphoreType.DMA((2,)),
        ],
        compiler_params=pltpu.CompilerParams(vmem_limit_bytes=8 * 1024 * 1024),
        name="finish_blocks",
    )(pair_table, *kept)


def solution(mesh):
    return jax.shard_map(
        per_device,
        mesh=mesh,
        in_specs=(P("win", None, None, "chan"), P("win"), P()),
        out_specs=P("win", None, "chan", None),
        check_vma=False,
    )
```

time: 132 us -> 115 us (0.87)
  Pallas kernels: 122 us -> 112 us
  other arithmetic: 7.08 us -> 0 us
    pallas_call x2, Pallas kernels: 122 us -> 112 us  [the longest x1 104 us: per_device(): pl.pallas_call(gather_stack_kernel, out_shape=[pltpu.VMEM((NBLK, GROUPS,...]
    transpose x1 -> x0, other arithmetic: 3.3 us -> none  [per_device(): tempered = tempered.transpose(1, 2, 0, 3).reshape(bins, chunk_rows, width)]
    reduce_sum x1 -> x0, other arithmetic: 3.11 us -> none  [per_device(): band = jnp.mean(raw * raw, axis=(1, 2), keepdims=True)]
    unnamed x0 -> x6, local copies, waits for them, and re-layouts: none -> 2.74 us
    transpose x1 -> x0, local copies, waits for them, and re-layouts: 2.43 us -> none  [per_device(): tempered = tempered.transpose(1, 2, 0, 3).reshape(bins, chunk_rows, width)]
where the time goes in v2:
time: 115 us
  Pallas kernels  112 us (97%)
  local copies, waits for them, and re-layouts  2.74 us (2%)
    pallas_call x1, Pallas kernels, per_device(): pl.pallas_call(gather_stack_kernel, out_shape=[pltpu.VMEM((NBLK, GROUPS,...  104 us
    pallas_call x1, Pallas kernels, per_device(): pl.pallas_call(functools.partial(finish_kernel, windows=windows), out_sha...  8.53 us
    unnamed x6, local copies, waits for them, and re-layouts  2.74 us

profile of v2, /device:TPU:1, one launch (start us, length us, event | category | flops | bytes accessed | tf_op | source)
XLA Modules:
  0.0 115.2 jit_solution(12818879897397337667)
XLA Ops:
  0.0 0.0 copy-start
  0.0 1.4 %copy-done = bf16[24,32,2,512]{3,2,1,0:T(2,128)(2,1)S(1)} copy-done((bf16[24,32,2,512]{3,2,1,0:T(2,128)(2,1)S(1)}, bf16[24,32,2,512]{3,2,1,0:T(2,128)(2,1)}, u32[]{:S(2)}) %copy-start) | copy-done | bytes 1572888
  1.4 0.0 copy-start.2
  1.4 0.7 copy-done.2
  2.1 104.0 %gather_stack.1 = (bf16[8,8,192,512]{3,2,1,0:T(8,128)(2,1)S(1)}, f32[8,2,512,512]{3,2,1,0:T(8,128)S(1)}, bf16[1024,384]{1,0:T(8,128)(2,1)S(1)}, f32[8,8,512]{2,1,0:T(8,128)S(1)}, f32[512,128]{1,0:T(8,128)S(1)}) custom-call(s32[24]{0:T(128)S(1)} %copy-done.2, bf16[24,256,128]{2,1,0:T(8,128)(2,1)S(1)} %bitcast.5), custom_call_target="tpu_custom_call" | custom-call | tf_op jit(solution)/shard_map/gather_stack/pallas_call | solution.py:311
  106.0 0.0 copy-start.1
  106.0 0.7 copy-done.1
  106.7 8.5 %finish_blocks.1 = bf16[1,2,512,4096]{3,2,1,0:T(8,128)(2,1)} custom-call(s32[8,8]{1,0:T(8,128)S(1)} %copy-done.1, bf16[8,8,192,512]{3,2,1,0:T(8,128)(2,1)S(1)} %get-tuple-element.10.x_all, f32[8,2,512,512]{3,2,1,0:T(8,128)S(1)} %get-tuple-element.11.acc, bf16[1024,384]{1,0:T(8,128)(2,1)S(1)} %get-tuple-element.12.left, ...), custom_call_target="tpu_custom_call" | custom-call | tf_op jit(solution)/shard_map/finish_blocks/pallas_call | solution.py:339
Async XLA Ops:
  0.0 1.4 %copy-start = (bf16[24,32,2,512]{3,2,1,0:T(2,128)(2,1)S(1)}, bf16[24,32,2,512]{3,2,1,0:T(2,128)(2,1)}, u32[]{:S(2)}) copy-start(bf16[24,32,2,512]{3,2,1,0:T(2,128)(2,1)} %param.3) | copy-start | bytes 4718596
  1.4 0.7 copy-start.2
  106.0 0.7 copy-start.1

commit v3 on v2

v3 whole, which is shorter than its diff:
```python
import functools
import math

import jax
import jax.numpy as jnp
from jax import lax
from jax.experimental import pallas as pl
from jax.experimental.pallas import tpu as pltpu
from jax.sharding import PartitionSpec as P

EPSILON = 1e-05
MESH = pl.DeviceIdType.MESH

NX = 4
NZ = 8
GROUPS = 8
OFFSETS = (0, -1, 1, -2, 2, -3, 3, 4)
NBLK = 8
HALF = 96
CUT_LO = 64
CUT_HI = (144, 160, 144, 160, 144, 160, 144, 144)
FIRST_LATE = 4
PAIR = 2
STACK_AT = (1, 3, 5, 7)
DEAL_FIRST = ((0, 0), (0, 1), (1, 0), (1, 1), (2, 0), (2, 1))
DEAL_LATER = (((3, 0), (4, 0)), ((3, 1), (4, 1)), ((5, 0), (6, 0)), ((5, 1), (6, 1)), ((7, 0),), ((7, 1),))
LOADS = 4


def block_rows(x_all, b, g0, groups):
    other = b + 1 - 2 * (b % 2)
    rows, width = groups * HALF, x_all.shape[3]
    same = x_all[b, g0 : g0 + groups, 0:HALF, :].reshape(rows, width)
    cross = x_all[other, g0 : g0 + groups, HALF : 2 * HALF, :].reshape(rows, width)
    return jnp.concatenate([same, cross], axis=0)


def build_left(x_all, own, g0, groups, chunk_rows, left, rowpow, first):
    rows, width = 2 * groups * HALF, x_all.shape[3]
    mine = block_rows(x_all, own, g0, groups).astype(jnp.float32)
    parts = mine.reshape(rows // chunk_rows, chunk_rows, width)
    h = chunk_rows // 2
    swapped = jnp.concatenate([parts[:, h:, :], -parts[:, :h, :]], axis=1).reshape(rows, width)
    re_t = mine.T
    left[0:width, 0:rows] = re_t.astype(jnp.bfloat16)
    left[width:, 0:rows] = swapped.T.astype(jnp.bfloat16)
    squares = re_t * re_t
    lanes = squares[:, 0:128]
    for k in range(128, rows, 128):
        lanes = lanes + squares[:, k : k + 128]
    rowpow[...] = lanes if first else rowpow[...] + lanes


def squares_of(right):
    wide = right.astype(jnp.float32)
    return jnp.sum((wide * wide).reshape(right.shape[0] // 8, 8, right.shape[1]), axis=0)


def gather_stack_kernel(
    flags_hbm,
    spectra_hbm,
    prod,
    x_tail,
    acc_tail,
    left,
    colpow,
    rowpow,
    x_all,
    acc,
    flags,
    spectra,
    wide,
    tempered,
    in_sem,
    ready,
    a2a_send,
    a2a_recv,
    near_recv,
    local_sem,
    ag_send,
    recv1,
    recv2,
    recv3,
):
    local_windows = spectra.shape[0]
    bins = wide.shape[0]
    batch = local_windows // LOADS
    loads = [pltpu.make_async_copy(flags_hbm, flags, in_sem.at[LOADS])]
    for i in range(LOADS):
        part = pl.ds(i * batch, batch)
        loads.append(pltpu.make_async_copy(spectra_hbm.at[part], spectra.at[part], in_sem.at[i]))
    for load in loads:
        load.start()
    chunk_rows = tempered.shape[1]
    c = lax.axis_index("chan")
    w = lax.axis_index("win")
    x, yl = c // 2, c % 2
    yh, z, core = w // 16, (w // 2) % NZ, w % 2
    xp = (x + 1 + 2 * core) % NX
    xm = (x + 3 + 2 * core) % NX
    x2 = (x + 2) % NX

    def src(xx, yy):
        return 2 * xx + yy

    own = src(x, yl)
    pair = src(x, 1 - yl)
    dev_p = (src(xp, yl), w)
    dev_m = (src(xm, yl), w)
    dev_y = (pair, w)

    def peer(zz, other_half, other_core):
        cc = c if not other_half else pair
        hh = yh if not other_half else 1 - yh
        kk = core if not other_core else 1 - core
        return (cc, hh * 16 + zz * 2 + kk)

    barrier = pltpu.get_barrier_semaphore()

    def greet(sems, zz):
        for other_half in (0, 1):
            for other_core in (0, 1):
                pl.semaphore_signal(
                    sems[other_half], inc=1, device_id=peer(zz, other_half, other_core), device_id_type=MESH
                )

    near = [peer(z, 0, 1), peer(z, 1, 0), peer(z, 1, 1), dev_p, dev_m, dev_y]
    for dev in near:
        pl.semaphore_signal(barrier, inc=1, device_id=dev, device_id_type=MESH)
    for k in range(1, NZ):
        zz = (z + k) % NZ

        @pl.when((zz > z) | (zz >= FIRST_LATE) & (z >= FIRST_LATE))
        def _():
            greet((barrier, barrier), zz)

    odd = lax.broadcasted_iota(jnp.int32, (8, 128), 0) % 2

    def temper(i, carry):
        raw = spectra[i].astype(jnp.float32).reshape(bins, 8, 128)
        power = jnp.sum(raw * raw, axis=0)
        power = power + jnp.where(odd == 0, pltpu.roll(power, 7, 0), pltpu.roll(power, 1, 0))
        scale = lax.rsqrt(power * (1.0 / (2 * bins)) + EPSILON) * flags[i].astype(jnp.float32)
        wide[:, pl.ds(pl.multiple_of(i * 8, 8), 8), :] = raw * scale
        return carry

    loads[0].wait()
    for i in range(LOADS):
        loads[i + 1].wait()
        lax.fori_loop(i * batch, (i + 1) * batch, temper, 0)
        if i == LOADS // 2 - 1:
            pl.semaphore_wait(barrier, len(near) + 4 * jnp.where(z < FIRST_LATE, z, NZ - 1))
            for k in range(1, NZ):

                zz = (z - k) % NZ

                @pl.when((zz < z) & (zz < FIRST_LATE))
                def _():
                    greet((ready.at[0, z], ready.at[1, z]), zz)

    def arrange(b):
        for tile in range(4):
            re = wide[b, pl.ds(2 * tile, local_windows, stride=8), :]
            im = wide[b, pl.ds(2 * tile + 1, local_windows, stride=8), :]
            both = jnp.concatenate([re, im], axis=0)
            tempered[b, :, tile * 128 : (tile + 1) * 128] = both.astype(jnp.bfloat16)

    local_row = pl.multiple_of(core * chunk_rows, 16)
    local = pltpu.make_async_copy(
        tempered.at[w], x_all.at[own, 0, pl.ds(local_row, chunk_rows)], local_sem
    )

    def deal(g, other_half):
        zz = (z - OFFSETS[g]) % NZ

        @pl.when((zz > z) & (z < FIRST_LATE))
        def _():
            pl.semaphore_wait(ready.at[other_half, zz], 2)

        for other_core in (0, 1):
            dev = peer(zz, other_half, other_core)
            arrange(dev[1])
            if g == 0 and not other_half and not other_core:
                local.start()
                continue
            row = pl.multiple_of(other_half * HALF + core * chunk_rows, 16)
            pltpu.make_async_remote_copy(
                src_ref=tempered.at[dev[1]],
                dst_ref=x_all.at[own if not other_half else pair, g, pl.ds(row, chunk_rows)],
                send_sem=a2a_send,
                recv_sem=a2a_recv.at[g] if g or other_half else near_recv,
                device_id=dev,
                device_id_type=MESH,
            ).start()

    def send(s, g, lo, hi, recv_sem, dev):
        ref = x_all.at[s, g, pl.ds(lo, hi - lo)]
        pltpu.make_async_remote_copy(
            src_ref=ref,
            dst_ref=ref,
            send_sem=ag_send,
            recv_sem=recv_sem,
            device_id=dev,
            device_id_type=MESH,
        ).start()

    def await_rows(rows, sem):
        ref = x_all.at[0, 0, pl.ds(0, rows)]
        pltpu.make_async_copy(ref, ref, sem).wait()

    full = 2 * HALF

    def phase1(g):
        cuts = [0, full]
        if g == 0:
            local.wait()
            await_rows(HALF - chunk_rows, near_recv)
            cuts = [0, HALF, full]
        for lo, hi in zip(cuts, cuts[1:]):
            if hi == full:
                await_rows(HALF if g == 0 else full, a2a_recv.at[g])
            send(own, g, lo, hi, recv1.at[g, 0], dev_p)
            send(own, g, lo, hi, recv1.at[g, 1], dev_m)
            send(own, g, lo, hi, recv1.at[g, 2], dev_y)

    def phase2(g):
        s_m, s_p = src(xm, yl), src(xp, yl)
        await_rows(full, recv1.at[g, 0])
        send(s_m, g, 0, HALF, recv2.at[g, 0], dev_p)
        await_rows(full, recv1.at[g, 1])
        send(s_p, g, HALF, full, recv2.at[g, 1], dev_m)
        send(s_m, g, CUT_LO, CUT_HI[g], recv2.at[g, 2], dev_y)
        send(s_p, g, CUT_LO, CUT_HI[g], recv2.at[g, 3], dev_y)
        await_rows(full, recv1.at[g, 2])
        send(pair, g, 0, CUT_LO, recv2.at[g, 4], dev_p)
        send(pair, g, CUT_HI[g], full, recv2.at[g, 5], dev_m)
        send(pair, g, CUT_HI[g], full, recv2.at[g, 6], dev_p)
        send(pair, g, 0, CUT_LO, recv2.at[g, 7], dev_m)

    def phase3(g):
        s_m, s_p = src(xm, 1 - yl), src(xp, 1 - yl)
        cut = CUT_HI[g] - CUT_LO
        await_rows(HALF, recv2.at[g, 0])
        await_rows(HALF, recv2.at[g, 1])
        send(src(x2, yl), g, CUT_LO, CUT_HI[g], recv3.at[g, 0], dev_y)
        await_rows(CUT_LO, recv2.at[g, 4])
        send(s_m, g, 0, CUT_LO, recv3.at[g, 1], dev_p)
        await_rows(full - CUT_HI[g], recv2.at[g, 5])
        send(s_p, g, CUT_HI[g], full, recv3.at[g, 2], dev_m)
        await_rows(cut, recv2.at[g, 2])
        await_rows(cut, recv2.at[g, 3])
        await_rows(full - CUT_HI[g], recv2.at[g, 6])
        await_rows(CUT_LO, recv2.at[g, 7])

    def arrived(g):
        await_rows(CUT_HI[g] - CUT_LO, recv3.at[g, 0])
        await_rows(CUT_LO, recv3.at[g, 1])
        await_rows(full - CUT_HI[g], recv3.at[g, 2])

    width = x_all.shape[3]
    mean = 1.0 / (2 * bins * local_windows)
    rows = PAIR * full

    def b_of(i, column):
        return src((column + 2 * (i // 2)) % NX, i % 2)

    def stack(column, count, g0):
        first, last = g0 == 0, g0 == GROUPS - PAIR
        far = column is x2
        sums = acc_tail if far else acc

        def body(i, carry):
            k = i if far else b_of(i, column)
            b = b_of(i, column)
            right = block_rows(x_all, b, g0, PAIR)
            power = squares_of(right)
            if not first:
                power = power + colpow[b]
            if last:
                col = lax.rsqrt(jnp.sum(power, axis=0, keepdims=True) * mean + EPSILON)
            else:
                colpow[b] = power

            def half(part, inner):
                product = jnp.dot(
                    left[pl.ds(pl.multiple_of(part * width, width), width), :],
                    block_rows(x_all, b, g0, PAIR),
                    preferred_element_type=jnp.float32,
                )
                if not first:
                    product = product + sums[k, part]
                if last:
                    prod[b, part] = (product * rowpow[:, 0:1] * col).astype(jnp.bfloat16)
                else:
                    sums[k, part] = product
                return inner

            lax.fori_loop(0, 2, half, 0)
            return carry

        lax.fori_loop(0, 2 * count, body, 0)

    for g, half in DEAL_FIRST:
        deal(g, half)
    for it in range(GROUPS + 3):
        if it < GROUPS:
            phase1(it)
        for g, half in DEAL_LATER[it] if it < len(DEAL_LATER) else ():
            deal(g, half)
        if 1 <= it < GROUPS + 1:
            phase2(it - 1)
        if 2 <= it < GROUPS + 2:
            phase3(it - 2)
        if it >= 3:
            arrived(it - 3)
            if it - 3 in STACK_AT and it < GROUPS + 2:
                stack(x2, 1, it - 3 - PAIR + 1)
        if it - 1 in STACK_AT:
            g0 = it - PAIR
            build_left(x_all, own, g0, PAIR, chunk_rows, left, rowpow, g0 == 0)
            if g0 == GROUPS - PAIR:
                row = lax.rsqrt(jnp.sum(rowpow[...], axis=1, keepdims=True) * mean + EPSILON)
                row = row * (1.0 / math.sqrt(bins * local_windows))
                rowpow[...] = jnp.broadcast_to(row, rowpow.shape)
            stack(x, 1, g0)
        if it - 2 in STACK_AT:
            stack((x + 1) % NX, 2, it - 2 - PAIR + 1)

    tails = [
        pltpu.make_async_copy(
            x_all.at[src(x2, i), pl.ds(GROUPS - PAIR, PAIR)], x_tail.at[i], in_sem.at[i]
        )
        for i in (0, 1)
    ]
    for tail in tails:
        tail.start()
    for tail in tails:
        tail.wait()
    sent = tempered.at[0:31]
    pltpu.make_async_copy(sent, sent, a2a_send).wait()
    sent = x_all.at[0:7]
    pltpu.make_async_copy(sent, sent, ag_send).wait()


def finish_kernel(
    table_hbm, prod_in, x_tail, acc_tail, left, colpow, rowpow, out, table, buf, sem, table_sem, *, windows
):
    c = lax.axis_index("chan")
    load = pltpu.make_async_copy(table_hbm, table, table_sem)
    load.start()
    width = x_tail.shape[3]
    mean = 1.0 / (2 * windows)
    column = (c // 2 + 2) % NX

    def copy(s, ref):
        return pltpu.make_async_copy(ref, out.at[0, :, :, pl.ds(s * width, width)], sem.at[s])

    def complete(i, carry):
        b = 2 * column + i
        right = block_rows(x_tail, i, 0, PAIR)
        power = jnp.sum(colpow[b] + squares_of(right), axis=0, keepdims=True)
        col = lax.rsqrt(power * mean + EPSILON)
        for part in (0, 1):
            product = jnp.dot(
                left[part * width : (part + 1) * width, :], right, preferred_element_type=jnp.float32
            )
            product = product + acc_tail[i, part]
            buf[i, part] = (product * rowpow[:, 0:1] * col).astype(jnp.bfloat16)
        return carry

    load.wait()
    for s in range(NBLK):
        b = table[c, s]

        @pl.when(b // 2 != column)
        def _():
            copy(s, prod_in.at[b]).start()

    lax.fori_loop(0, 2, complete, 0)
    for s in range(NBLK):
        b = table[c, s]

        @pl.when(b // 2 == column)
        def _():
            copy(s, buf.at[b % 2]).start()

    for s in range(NBLK):
        copy(s, buf.at[0]).wait()


def at_home(array):
    return pltpu.with_memory_space_constraint(array, pltpu.HBM)


def per_device(spectra, flags, pair_table):
    local, bins, parts, width = spectra.shape
    windows = local * lax.axis_size("win")
    chunk_rows = local * parts
    tiles = width // 128
    rows = spectra.reshape(local, bins, parts, tiles, 128).transpose(0, 1, 3, 2, 4)
    rows = rows.reshape(local, bins * tiles * parts, 128)

    vmem = pl.BlockSpec(memory_space=pltpu.VMEM)
    hbm = pl.BlockSpec(memory_space=pltpu.HBM)
    kept = pl.pallas_call(
        gather_stack_kernel,
        out_shape=[
            pltpu.VMEM((NBLK, 2, width, width), jnp.bfloat16),
            pltpu.VMEM((2, PAIR, 2 * HALF, width), jnp.bfloat16),
            pltpu.VMEM((2, 2, width, width), jnp.float32),
            pltpu.VMEM((2 * width, PAIR * 2 * HALF), jnp.bfloat16),
            pltpu.VMEM((NBLK, 8, width), jnp.float32),
            pltpu.VMEM((width, 128), jnp.float32),
        ],
        in_specs=[hbm, hbm],
        out_specs=[vmem] * 6,
        scratch_shapes=[
            pltpu.VMEM((NBLK, GROUPS, 2 * HALF, width), jnp.bfloat16),
            pltpu.VMEM((NBLK, 2, width, width), jnp.float32),
            pltpu.SMEM((local,), jnp.int32),
            pltpu.VMEM(rows.shape, jnp.bfloat16),
            pltpu.VMEM((bins, local * 8, 128), jnp.float32),
            pltpu.VMEM((bins, chunk_rows, width), jnp.bfloat16),
            pltpu.SemaphoreType.DMA((LOADS + 1,)),
            pltpu.SemaphoreType.REGULAR((2, NZ)),
            pltpu.SemaphoreType.DMA,
            pltpu.SemaphoreType.DMA((GROUPS,)),
            pltpu.SemaphoreType.DMA,
            pltpu.SemaphoreType.DMA,
            pltpu.SemaphoreType.DMA,
            pltpu.SemaphoreType.DMA((GROUPS, 3)),
            pltpu.SemaphoreType.DMA((GROUPS, 8)),
            pltpu.SemaphoreType.DMA((GROUPS, 3)),
        ],
        compiler_params=pltpu.CompilerParams(
            collective_id=0, has_side_effects=True, vmem_limit_bytes=40 * 1024 * 1024
        ),
        name="gather_stack",
    )(at_home(flags), at_home(rows))

    return pl.pallas_call(
        functools.partial(finish_kernel, windows=windows),
        out_shape=jax.ShapeDtypeStruct((1, 2, width, NBLK * width), jnp.bfloat16),
        in_specs=[hbm] + [vmem] * 6,
        out_specs=pl.BlockSpec(memory_space=pltpu.HBM),
        scratch_shapes=[
            pltpu.SMEM(pair_table.shape, jnp.int32),
            pltpu.VMEM((2, 2, width, width), jnp.bfloat16),
            pltpu.SemaphoreType.DMA((NBLK,)),
            pltpu.SemaphoreType.DMA,
        ],
        compiler_params=pltpu.CompilerParams(vmem_limit_bytes=8 * 1024 * 1024),
        name="finish_blocks",
    )(at_home(pair_table), *kept)


def solution(mesh):
    return jax.shard_map(
        per_device,
        mesh=mesh,
        in_specs=(P("win", None, None, "chan"), P("win"), P()),
        out_specs=P("win", None, "chan", None),
        check_vma=False,
    )
```

time: 115 us -> 103 us (0.90)
  Pallas kernels: 112 us -> 103 us
  local copies, waits for them, and re-layouts: 2.74 us -> 0 us
    pallas_call x1, Pallas kernels: 104 us -> 98.5 us  [per_device(): pl.pallas_call(gather_stack_kernel, out_shape=[pltpu.VMEM((NBLK, 2, width...]
    pallas_call x1, Pallas kernels: 8.53 us -> 4.12 us  [per_device(): pl.pallas_call(functools.partial(finish_kernel, windows=windows), out_sha...]
    unnamed x6 -> x0, local copies, waits for them, and re-layouts: 2.74 us -> none
where the time goes in v3:
time: 103 us
  Pallas kernels  103 us (100%)
    pallas_call x1, Pallas kernels, per_device(): pl.pallas_call(gather_stack_kernel, out_shape=[pltpu.VMEM((NBLK, 2, width...  98.5 us
    pallas_call x1, Pallas kernels, per_device(): pl.pallas_call(functools.partial(finish_kernel, windows=windows), out_sha...  4.12 us

profile of v3, /device:TPU:1, one launch (start us, length us, event | category | flops | bytes accessed | tf_op | source)
XLA Modules:
  0.0 102.7 jit_solution(7893161270083237876)
XLA Ops:
  0.0 98.5 %gather_stack.1 = (bf16[8,2,512,512]{3,2,1,0:T(8,128)(2,1)S(1)}, bf16[2,2,192,512]{3,2,1,0:T(8,128)(2,1)S(1)}, f32[2,2,512,512]{3,2,1,0:T(8,128)S(1)}, bf16[1024...) custom-call(s32[24]{0:T(128)} %flags_hbm.1, bf16[24,256,128]{2,1,0:T(8,128)(2,1)} %bitcast.5), custom_call_target="tpu_custom_call" | custom-call | tf_op jit(solution)/shard_map/gather_stack/pallas_call | solution.py:405
  98.5 4.1 %finish_blocks.1 = bf16[1,2,512,4096]{3,2,1,0:T(8,128)(2,1)} custom-call(s32[8,8]{1,0:T(8,128)} %table_hbm.1, bf16[8,2,512,512]{3,2,1,0:T(8,128)(2,1)S(1)} %get-tuple-element.11.prod_in, bf16[2,2,192,512]{3,2,1,0:T(8,128)(2,1)S(1)} %get-tuple-element.12.x_tail, f32[2,2,512,512]{3,2,1,0:T(8,128)S(1)} %get-tuple-element.13.acc_tail, ...), custom_call_target="tpu_custom_call" | custom-call | tf_op jit(solution)/shard_map/finish_blocks/pallas_call | solution.py:441

commit v4 on v3

--- a/solution.py
+++ b/solution.py
@@ -172,6 +172,7 @@
 
     def deal(g, other_half):
         zz = (z - OFFSETS[g]) % NZ
+        slot = jnp.where(zz == 0, 3 - g, g) if g in (1, 2) else g
 
         @pl.when((zz > z) & (z < FIRST_LATE))
         def _():
@@ -186,9 +187,9 @@
             row = pl.multiple_of(other_half * HALF + core * chunk_rows, 16)
             pltpu.make_async_remote_copy(
                 src_ref=tempered.at[dev[1]],
-                dst_ref=x_all.at[own if not other_half else pair, g, pl.ds(row, chunk_rows)],
+                dst_ref=x_all.at[own if not other_half else pair, slot, pl.ds(row, chunk_rows)],
                 send_sem=a2a_send,
-                recv_sem=a2a_recv.at[g] if g or other_half else near_recv,
+                recv_sem=a2a_recv.at[slot] if g or other_half else near_recv,
                 device_id=dev,
                 device_id_type=MESH,
             ).start()

time: 103 us -> 102 us (level)
  Pallas kernels: 103 us -> 101 us
    pallas_call x1, Pallas kernels: 98.5 us -> 97 us  [per_device(): pl.pallas_call(gather_stack_kernel, out_shape=[pltpu.VMEM((NBLK, 2, width...]
where the time goes in v4:
time: 102 us; the launch traced here: 101 us
  Pallas kernels  101 us (99%)
    pallas_call x1, Pallas kernels, per_device(): pl.pallas_call(gather_stack_kernel, out_shape=[pltpu.VMEM((NBLK, 2, width...  97 us
    pallas_call x1, Pallas kernels, per_device(): pl.pallas_call(functools.partial(finish_kernel, windows=windows), out_sha...  4.11 us

profile of v4, /device:TPU:1, one launch (start us, length us, event | category | flops | bytes accessed | tf_op | source)
XLA Modules:
  0.0 101.2 jit_solution(12962352019938541016)
XLA Ops:
  0.0 97.0 %gather_stack.1 = (bf16[8,2,512,512]{3,2,1,0:T(8,128)(2,1)S(1)}, bf16[2,2,192,512]{3,2,1,0:T(8,128)(2,1)S(1)}, f32[2,2,512,512]{3,2,1,0:T(8,128)S(1)}, bf16[1024...) custom-call(s32[24]{0:T(128)} %flags_hbm.1, bf16[24,256,128]{2,1,0:T(8,128)(2,1)} %bitcast.5), custom_call_target="tpu_custom_call" | custom-call | tf_op jit(solution)/shard_map/gather_stack/pallas_call | solution.py:406
  97.0 4.1 %finish_blocks.1 = bf16[1,2,512,4096]{3,2,1,0:T(8,128)(2,1)} custom-call(s32[8,8]{1,0:T(8,128)} %table_hbm.1, bf16[8,2,512,512]{3,2,1,0:T(8,128)(2,1)S(1)} %get-tuple-element.11.prod_in, bf16[2,2,192,512]{3,2,1,0:T(8,128)(2,1)S(1)} %get-tuple-element.12.x_tail, f32[2,2,512,512]{3,2,1,0:T(8,128)S(1)} %get-tuple-element.13.acc_tail, ...), custom_call_target="tpu_custom_call" | custom-call | tf_op jit(solution)/shard_map/finish_blocks/pallas_call | solution.py:442
